TPU v7x, 512 devices: a whole 4x8x8 slice. The times are simulated.
512 devices in a mesh: group: 16 (over y, core), inner: 32 (over x, z).
Axes of the slice: x: 4, y: 8, z: 8, core: 2. Of those that a mesh axis runs over, the one named last changes fastest.
Arguments:
- pair_rows: bfloat16 [8192, 2048], P(('group', 'inner')), may hold values from -6 to 6
- group_ids: int32 [8192, 1], P(('group', 'inner')), may hold values from 0 to 15; in each aligned block of 16 rows (0 to 15, 16 to 31, ...) at most 2 rows name the same one
- local_ids: int32 [8192, 1], P(('group', 'inner')), may hold values from 0 to 1
- route_weight: float32 [8192], P(('group', 'inner')), may hold values from 0.3 to 1
- w_up: bfloat16 [32, 2048, 8192], P('group', None, 'inner'), may hold values from -0.125 to 0.125
- w_down: bfloat16 [32, 8192, 2048], P('group', 'inner'), may hold values from -0.0625 to 0.0625
Outputs:
- mixed: bfloat16 [8192, 2048], P(('group', 'inner'))
Inputs may be any that keep to these rules, and one draw needn't show every extreme that they name: `group_ids`: among the rows of one device no value is named more than 2 times, a bound that some block reaches.
All inputs are finite; a program needn't handle non-finite values.
Results may differ from a plain program's by a relative error of at most 0.02.
Values may be sent and summed in bfloat16 or wider, within the bound.
A program may use at most 64 MiB of HBM per device.

v0:
```python
import jax
import jax.numpy as jnp
from jax import lax
from jax.sharding import PartitionSpec as P


def body(pair_rows, group_ids, local_ids, route_weight, w_up, w_down):
    groups = lax.axis_size("group")
    inner_size = lax.axis_size("inner")
    count_rows = pair_rows.shape[0]
    model_width = pair_rows.shape[1]
    local_count = w_up.shape[0]
    capacity = 2 * count_rows // groups
    group_of = group_ids[:, 0]
    onehot = (group_of[:, None] == jnp.arange(groups, dtype=jnp.int32)[None, :]).astype(jnp.int32)
    rank_in = jnp.sum((jnp.cumsum(onehot, 0) - onehot) * onehot, 1)
    target = group_of * capacity + rank_in
    placing = (jnp.arange(groups * capacity, dtype=jnp.int32)[:, None] == target[None, :]).astype(
        jnp.bfloat16
    )
    outgoing = jnp.dot(placing, pair_rows, preferred_element_type=jnp.float32).astype(jnp.bfloat16)
    outgoing = outgoing.reshape(1, groups, capacity, model_width)
    tag_rows = (local_ids[:, 0] + 1).astype(jnp.bfloat16)
    tags = jnp.dot(placing, tag_rows, preferred_element_type=jnp.float32).astype(jnp.bfloat16)
    tags = tags.reshape(1, groups, capacity)
    arrived, arrived_tags = (
        lax.all_to_all(outgoing, "group", split_axis=1, concat_axis=1, tiled=True),
        lax.all_to_all(tags, "group", split_axis=1, concat_axis=1, tiled=True),
    )
    gathered, gathered_tags = (
        lax.all_gather(arrived, "inner", axis=0, tiled=True),
        lax.all_gather(arrived_tags, "inner", axis=0, tiled=True),
    )
    slots = gathered.reshape(inner_size * groups * capacity, model_width)
    slot_tags = gathered_tags.reshape(inner_size * groups * capacity).astype(jnp.float32)
    expert_index = jnp.arange(local_count, dtype=jnp.float32) + 1.0
    own_rows = groups * capacity
    selector = (slot_tags[:, None] == expert_index[None, :]).astype(jnp.float32)
    up_val = jnp.einsum("rd,edf->ref", slots, w_up, preferred_element_type=jnp.float32)
    hidden = (jax.nn.silu(up_val) * selector[:, :, None]).astype(jnp.bfloat16)
    every_term = jnp.einsum("ref,efd->rd", hidden, w_down, preferred_element_type=jnp.float32)
    totals = lax.psum(every_term.astype(jnp.bfloat16), "inner").astype(jnp.float32)
    summed = lax.dynamic_slice_in_dim(totals, lax.axis_index("inner") * own_rows, own_rows, 0)
    send_back = summed.astype(jnp.bfloat16).reshape(groups, capacity, model_width)
    returned = lax.all_to_all(send_back, "group", split_axis=0, concat_axis=0, tiled=True)
    combined = jnp.dot(
        placing.T,
        returned.reshape(groups * capacity, model_width),
        preferred_element_type=jnp.float32,
    )
    return (combined * route_weight[:, None]).astype(jnp.bfloat16)


def solution(mesh):
    placed = (
        P(("group", "inner"), None),
        P(("group", "inner"), None),
        P(("group", "inner"), None),
        P(("group", "inner")),
        P("group", None, "inner"),
        P("group", "inner", None),
    )
    return jax.shard_map(
        body, mesh=mesh, in_specs=placed, out_specs=P(("group", "inner"), None), check_vma=False
    )
```

profile of v0, /device:TPU:1, one launch (start us, length us, event | category | flops | bytes accessed | tf_op | source)
XLA Modules:
  0.0 338.9 jit_solution(1572055282033931939)
XLA Ops:
  6.5 0.9 fusion.5
  7.5 0.8 select_reduce_fusion
  8.3 0.7 multiply_add_fusion
  9.0 1.0 convolution_convert_fusion
  10.0 0.1 reshape.67
  10.1 18.5 %all_to_all.15 = bf16[1,16,2,2048]{3,2,0,1:T(2,128)(2,1)S(1)} all-to-all(bf16[1,16,2,2048]{3,2,0,1:T(2,128)(2,1)S(1)} %bitcast.15), channel_id=1, replica_groups=mesh['group'=16,'inner'=32] {'group'}, dimensions={1} | all-to-all | bytes 262144 | tf_op jit(solution)/shard_map/all_to_all | solution.py:27
  28.6 0.7 copy.14
  29.3 0.8 fusion.1
  30.1 0.7 reshape.78
  30.8 3.4 all-to-all-start.1
  34.2 6.5 %all-to-all-done.1 = bf16[1,16,2]{2,0,1:T(2,128)(2,1)S(1)} async-done(((bf16[1,16,2]{2,0,1:T(2,128)(2,1)}), bf16[1,16,2]{2,0,1:T(2,128)(2,1)S(1)}, u32[]{:S(2)}, u32[]{:S(2)}) %all-to-all-start.1) | async-done | bytes 96 | tf_op jit(solution)/shard_map/all_to_all | solution.py:28
  40.7 0.1 copy.17
  40.8 37.2 %all_gather.7 = bf16[32,16,2]{1,2,0:T(2,128)(2,1)S(1)} all-gather(bf16[1,16,2]{1,2,0:T(2,128)(2,1)S(1)} %copy.17), channel_id=1, replica_groups=mesh['group'=16,'inner'=32] {'inner'}, dimensions={0}, use_global_device_ids=true | all-gather | bytes 2112 | tf_op jit(solution)/shard_map/all_gather | solution.py:32
  78.1 0.2 copy.19
  78.3 0.2 reshape.72
  78.5 34.5 %all-gather.2.cloned.1.call-done = bf16[32,16,2,2048]{3,1,2,0:T(8,128)(2,1)} async-done(((bf16[1,16,2,2048]{3,1,2,0:T(8,128)(2,1)}), bf16[32,16,2,2048]{3,1,2,0:T(8,128)(2,1)}) %all-gather.2.cloned.1.call-update) | async-done | bytes 4194320 | tf_op jit(solution)/shard_map/all_gather | solution.py:31
  113.1 8.5 %copy.15 = bf16[32,16,2,2048]{3,2,1,0:T(2,128)(2,1)} copy(bf16[32,16,2,2048]{3,1,2,0:T(8,128)(2,1)} %all-gather.2.cloned.1.call-done) | data formatting | bytes 8388608 | tf_op jit(solution)/shard_map/all_gather | solution.py:31
  121.6 7.2 %reshape.73 = bf16[1024,2048,1]{1,0,2:T(8,128)(2,1)} reshape(bf16[32,16,2,2048]{3,2,1,0:T(2,128)(2,1)} %copy.15) | data formatting | bytes 8388608 | tf_op jit(solution)/shard_map/reshape | solution.py:34
  128.8 9.5 %bitcast_convert_fusion = bf16[1024,2048]{1,0:T(8,128)(2,1)} fusion(bf16[2,256,2048]{2,1,0:T(8,128)(2,1)S(1)} %copy-done, bf16[1024,2048,1]{1,0,2:T(8,128)(2,1)} %reshape.73, bf16[2,2048,256]{2,1,0:T(8,128)(2,1)} %param.10, f32[1024,2]{0,1:T(2,128)S(1)} %compare_convert_fusion), kind=kOutput, calls=%fused_computation | convolution fusion | flops 4300210176 | bytes 12591104 | tf_op jit(solution)/shard_map/ref,efd->rd/dot_general | solution.py:41
  138.4 172.9 %all-reduce.2.cloned.1.call-done = bf16[1024,2048]{1,0:T(8,128)(2,1)} async-done(((bf16[1024,2048]{1,0:T(8,128)(2,1)}), bf16[1024,2048]{1,0:T(8,128)(2,1)}) %all-reduce.2.cloned.1.call-update) | async-done | bytes 4194320 | tf_op jit(solution)/shard_map/psum | solution.py:42
  311.2 0.9 convert_convert_fusion
  312.1 0.1 reshape.70
  312.2 19.0 %all_to_all.16 = bf16[16,2,2048]{2,1,0:T(2,128)(2,1)S(1)} all-to-all(bf16[16,2,2048]{2,1,0:T(2,128)(2,1)S(1)} %reshape.70), channel_id=1, replica_groups=mesh['group'=16,'inner'=32] {'group'}, dimensions={0} | all-to-all | bytes 262144 | tf_op jit(solution)/shard_map/all_to_all | solution.py:45
  331.3 0.8 fusion
  (13 shorter events, 0.3 us)
Async XLA Ops:
  6.5 122.3 %copy-start = (bf16[2,256,2048]{2,1,0:T(8,128)(2,1)S(1)}, bf16[2,256,2048]{2,1,0:T(8,128)(2,1)}, u32[]{:S(2)}) copy-start(bf16[2,256,2048]{2,1,0:T(8,128)(2,1)} %param.11) | copy-start | bytes 6291460
  6.5 106.6 %all-gather.2.cloned.1.call-start = ((), (), s32[]{:S(2)}) async-start(), calls=%async_computation.3 | async-start | bytes 4325376 | tf_op jit(solution)/shard_map/all_gather | solution.py:31
  30.8 9.9 %all-to-all-start.1 = ((bf16[1,16,2]{2,0,1:T(2,128)(2,1)}), bf16[1,16,2]{2,0,1:T(2,128)(2,1)S(1)}, u32[]{:S(2)}, u32[]{:S(2)}) async-start(bf16[1,16,2]{2,0,1:T(2,128)(2,1)} %reshape.78), calls=%async_computation.1 | async-start | bytes 16384 | tf_op jit(solution)/shard_map/all_to_all | solution.py:28
  34.1 277.1 %all-reduce.2.cloned.1.call-start = ((), (), s32[]{:S(2)}) async-start(), calls=%async_computation.4 | async-start | bytes 8388608 | tf_op jit(solution)/shard_map/psum | solution.py:42
  138.3 192.9 %copy-start.1 = (f32[16]{0:T(128)S(1)}, f32[16]{0:T(128)}, u32[]{:S(2)}) copy-start(f32[16]{0:T(128)} %param.9) | copy-start | bytes 196
Sparse Core Ops, SparseCore 0:
  29.4 83.6 all-gather.1
  138.5 172.6 all-reduce.1
where the time goes:
time: 339 us
  waiting for transfers between devices  214 us (63%)
  blocking collectives  74.7 us (22%)
  local copies, waits for them, and re-layouts  17.9 us (5%)
  between operations  13.5 us (4%)
  matrix products  12.1 us (4%)
  starting transfers between devices  3.41 us (1%)
  other arithmetic  3.41 us (1%)
    psum x1, waiting for transfers between devices, body(): lax.psum(every_term.astype(jnp.bfloat16), 'inner').astype(jnp.float32)  173 us
    all_gather x1, blocking collectives, body(): lax.all_gather(arrived_tags, 'inner', axis=0, tiled=True)  37.2 us
    all_gather x1, waiting for transfers between devices, body(): lax.all_gather(arrived, 'inner', axis=0, tiled=True)  34.5 us
    all_to_all x1, blocking collectives, body(): lax.all_to_all(send_back, 'group', split_axis=0, concat_axis=0, tiled=True)  19 us
    all_to_all x1, blocking collectives, body(): lax.all_to_all(outgoing, 'group', split_axis=1, concat_axis=1, tiled=True)  18.5 us
    dot_general x1, matrix products, body(): jnp.einsum('ref,efd->rd', hidden, w_down, preferred_element_type=jnp.floa...  9.51 us
    all_gather x1, local copies, waits for them, and re-layouts, body(): lax.all_gather(arrived, 'inner', axis=0, tiled=True)  8.52 us
    reshape x1, local copies, waits for them, and re-layouts, body(): slots = gathered.reshape(inner_size * groups * capacity, model_width)  7.19 us
  transfers between devices with their start and end apart: 3, of which 3 were waited for; matrix products, arithmetic and copies ran while one was open for 1% of the time, Pallas kernels for 0%

commit v1 on v0

--- a/solution.py
+++ b/solution.py
@@ -27,8 +27,13 @@
         lax.all_to_all(outgoing, "group", split_axis=1, concat_axis=1, tiled=True),
         lax.all_to_all(tags, "group", split_axis=1, concat_axis=1, tiled=True),
     )
+
+    def push_the_column(slab_in, which_dim):
+        r2 = jnp.stack([slab_in] * lax.axis_size("inner"), axis=0)
+        return jnp.concatenate(lax.all_to_all(r2, "inner", 0, 0), axis=which_dim)
+
     gathered, gathered_tags = (
-        lax.all_gather(arrived, "inner", axis=0, tiled=True),
+        push_the_column(arrived, which_dim=0),
         lax.all_gather(arrived_tags, "inner", axis=0, tiled=True),
     )
     slots = gathered.reshape(inner_size * groups * capacity, model_width)

time: 339 us -> 394 us (1.16)
  blocking collectives: 74.7 us -> 149 us
  waiting for transfers between devices: 214 us -> 178 us
  starting transfers between devices: 3.41 us -> 21.6 us
    all_gather x1, blocking collectives: 37.2 us -> 118 us  [body(): lax.all_gather(arrived_tags, 'inner', axis=0, tiled=True)]
    all_gather x1 -> x0, waiting for transfers between devices: 34.5 us -> none  [body(): lax.all_gather(arrived, 'inner', axis=0, tiled=True)]
    another operation x0 -> x2, local copies, waits for them, and re-layouts: none -> 13.1 us  [the longest x1 7.21 us: body(): slots = gathered.reshape(inner_size * groups * capacity, model_width)]
    all_to_all x0 -> x1, starting transfers between devices: none -> 11.4 us  [push_the_column(): return jnp.concatenate(lax.all_to_all(r2, 'inner', 0, 0), axis=which_dim)]
    all_gather x1 -> x0, local copies, waits for them, and re-layouts: 8.52 us -> none  [body(): lax.all_gather(arrived, 'inner', axis=0, tiled=True)]
    reshape x1 -> x0, local copies, waits for them, and re-layouts: 7.19 us -> none  [body(): slots = gathered.reshape(inner_size * groups * capacity, model_width)]
    all_to_all x1, starting transfers between devices: 3.37 us -> 10.1 us  [body(): lax.all_to_all(tags, 'group', split_axis=1, concat_axis=1, tiled=True)]
    all_to_all x1, blocking collectives: 18.5 us -> 12.3 us  [body(): lax.all_to_all(outgoing, 'group', split_axis=1, concat_axis=1, tiled=True)]
  transfers between devices with their start and end apart: 3 -> 3, of which waited for: 3 -> 2; matrix products, arithmetic and copies ran while one was open for 1% -> 0% of each run, Pallas kernels for 0% -> 0%
where the time goes in v1:
time: 394 us; the launch traced here: 393 us
  waiting for transfers between devices  178 us (45%)
  blocking collectives  149 us (38%)
  starting transfers between devices  21.6 us (5%)
  local copies, waits for them, and re-layouts  14.6 us (4%)
  between operations  13.5 us (3%)
  matrix products  12.1 us (3%)
    psum x1, waiting for transfers between devices, body(): lax.psum(every_term.astype(jnp.bfloat16), 'inner').astype(jnp.float32)  173 us
    all_gather x1, blocking collectives, body(): lax.all_gather(arrived_tags, 'inner', axis=0, tiled=True)  118 us
    all_to_all x1, blocking collectives, body(): lax.all_to_all(send_back, 'group', split_axis=0, concat_axis=0, tiled=True)  19 us
    all_to_all x1, blocking collectives, body(): lax.all_to_all(outgoing, 'group', split_axis=1, concat_axis=1, tiled=True)  12.3 us
    all_to_all x1, starting transfers between devices, push_the_column(): return jnp.concatenate(lax.all_to_all(r2, 'inner', 0, 0), axis=which_dim)  11.4 us
    all_to_all x1, starting transfers between devices, body(): lax.all_to_all(tags, 'group', split_axis=1, concat_axis=1, tiled=True)  10.1 us
    dot_general x1, matrix products, body(): jnp.einsum('ref,efd->rd', hidden, w_down, preferred_element_type=jnp.floa...  9.5 us
  transfers between devices with their start and end apart: 3, of which 2 were waited for; matrix products, arithmetic and copies ran while one was open for 0% of the time, Pallas kernels for 0%

profile of v1, /device:TPU:1, one launch (start us, length us, event | category | flops | bytes accessed | tf_op | source)
XLA Modules:
  0.0 393.1 jit_solution(7480798774100154387)
XLA Ops:
  6.5 0.9 fusion.5
  7.4 0.8 select_reduce_fusion
  8.3 0.7 multiply_add_fusion
  8.9 0.8 fusion.1
  9.7 0.7 reshape.77
  10.4 10.1 %all-to-all-start.2 = ((bf16[1,16,2]{2,0,1:T(2,128)(2,1)}), bf16[1,16,2]{2,0,1:T(2,128)(2,1)S(1)}, u32[]{:S(2)}, u32[]{:S(2)}) async-start(bf16[1,16,2]{2,0,1:T(2,128)(2,1)} %reshape.77), calls=%async_computation.2 | async-start | bytes 16384 | tf_op jit(solution)/shard_map/all_to_all | solution.py:28
  20.6 1.0 convolution_convert_fusion
  21.6 0.1 reshape.67
  21.7 5.9 %all-to-all-done.2 = bf16[1,16,2]{2,0,1:T(2,128)(2,1)S(1)} async-done(((bf16[1,16,2]{2,0,1:T(2,128)(2,1)}), bf16[1,16,2]{2,0,1:T(2,128)(2,1)S(1)}, u32[]{:S(2)}, u32[]{:S(2)}) %all-to-all-start.2) | async-done | bytes 96 | tf_op jit(solution)/shard_map/all_to_all | solution.py:28
  27.6 12.3 %all_to_all.23 = bf16[1,16,2,2048]{3,2,0,1:T(2,128)(2,1)S(1)} all-to-all(bf16[1,16,2,2048]{3,2,0,1:T(2,128)(2,1)S(1)} %bitcast.17), channel_id=1, replica_groups=mesh['group'=16,'inner'=32] {'group'}, dimensions={1} | all-to-all | bytes 262144 | tf_op jit(solution)/shard_map/all_to_all | solution.py:27
  39.8 5.9 %stack.2 = bf16[32,1,16,2,2048]{4,3,2,1,0:T(2,128)(2,1)} broadcast(bf16[16,2,2048]{2,1,0:T(2,128)(2,1)S(1)} %bitcast.16), dimensions={2,3,4} | broadcast | bytes 4325376 | tf_op jit(solution)/shard_map/stack | solution.py:32
  45.7 11.4 %all-to-all-start.1 = ((bf16[32,1,16,2,2048]{4,3,2,1,0:T(2,128)(2,1)}), bf16[32,1,16,2,2048]{4,3,2,1,0:T(2,128)(2,1)}, u32[]{:S(2)}, u32[]{:S(2)}) async-start(bf16[32,1,16,2,2048]{4,3,2,1,0:T(2,128)(2,1)} %stack.2), calls=%async_computation.1 | async-start | bytes 8388608 | tf_op jit(solution)/shard_map/all_to_all | solution.py:33
  57.2 0.1 copy.13
  57.3 118.1 %all_gather.3 = bf16[32,16,2]{1,2,0:T(2,128)(2,1)S(1)} all-gather(bf16[1,16,2]{1,2,0:T(2,128)(2,1)S(1)} %copy.13), channel_id=1, replica_groups=mesh['group'=16,'inner'=32] {'inner'}, dimensions={0}, use_global_device_ids=true | all-gather | bytes 2112 | tf_op jit(solution)/shard_map/all_gather | solution.py:37
  175.5 0.1 copy.14
  175.5 0.2 copy.15
  175.8 0.2 reshape.71
  176.0 7.2 %reshape.72 = bf16[1024,2048,1]{1,0,2:T(8,128)(2,1)} reshape(bf16[32,1,16,2,2048]{4,3,2,1,0:T(2,128)(2,1)} %all-to-all-done.1) | data formatting | bytes 8388608 | tf_op jit(solution)/shard_map/reshape;reshape | solution.py:39
  183.2 9.5 %bitcast_convert_fusion = bf16[1024,2048]{1,0:T(8,128)(2,1)} fusion(bf16[2,256,2048]{2,1,0:T(8,128)(2,1)S(1)} %copy-done, bf16[1024,2048,1]{1,0,2:T(8,128)(2,1)} %reshape.72, bf16[2,2048,256]{2,1,0:T(8,128)(2,1)} %param.10, f32[1024,2]{0,1:T(2,128)S(1)} %compare_convert_fusion), kind=kOutput, calls=%fused_computation | convolution fusion | flops 4300210176 | bytes 12591104 | tf_op jit(solution)/shard_map/ref,efd->rd/dot_general | solution.py:46
  192.7 172.6 %all-reduce.2.cloned.1.call-done = bf16[1024,2048]{1,0:T(8,128)(2,1)} async-done(((bf16[1024,2048]{1,0:T(8,128)(2,1)}), bf16[1024,2048]{1,0:T(8,128)(2,1)}) %all-reduce.2.cloned.1.call-update) | async-done | bytes 4194320 | tf_op jit(solution)/shard_map/psum | solution.py:47
  365.3 0.9 convert_convert_fusion
  366.2 0.1 reshape.69
  366.4 19.0 %all_to_all.24 = bf16[16,2,2048]{2,1,0:T(2,128)(2,1)S(1)} all-to-all(bf16[16,2,2048]{2,1,0:T(2,128)(2,1)S(1)} %reshape.69), channel_id=1, replica_groups=mesh['group'=16,'inner'=32] {'group'}, dimensions={0} | all-to-all | bytes 262144 | tf_op jit(solution)/shard_map/all_to_all | solution.py:50
  385.4 0.8 fusion
  (11 shorter events, 0.2 us)
Async XLA Ops:
  6.5 176.7 %copy-start = (bf16[2,256,2048]{2,1,0:T(8,128)(2,1)S(1)}, bf16[2,256,2048]{2,1,0:T(8,128)(2,1)}, u32[]{:S(2)}) copy-start(bf16[2,256,2048]{2,1,0:T(8,128)(2,1)} %param.11) | copy-start | bytes 6291460
  10.4 17.1 %all-to-all-start.2 = ((bf16[1,16,2]{2,0,1:T(2,128)(2,1)}), bf16[1,16,2]{2,0,1:T(2,128)(2,1)S(1)}, u32[]{:S(2)}, u32[]{:S(2)}) async-start(bf16[1,16,2]{2,0,1:T(2,128)(2,1)} %reshape.77), calls=%async_computation.2 | async-start | bytes 16384 | tf_op jit(solution)/shard_map/all_to_all | solution.py:28
  45.7 130.3 %all-to-all-start.1 = ((bf16[32,1,16,2,2048]{4,3,2,1,0:T(2,128)(2,1)}), bf16[32,1,16,2,2048]{4,3,2,1,0:T(2,128)(2,1)}, u32[]{:S(2)}, u32[]{:S(2)}) async-start(bf16[32,1,16,2,2048]{4,3,2,1,0:T(2,128)(2,1)} %stack.2), calls=%async_computation.1 | async-start | bytes 8388608 | tf_op jit(solution)/shard_map/all_to_all | solution.py:33
  57.2 308.2 %all-reduce.2.cloned.1.call-start = ((), (), s32[]{:S(2)}) async-start(), calls=%async_computation.4 | async-start | bytes 8388608 | tf_op jit(solution)/shard_map/psum | solution.py:47
  192.7 192.7 %copy-start.1 = (f32[16]{0:T(128)S(1)}, f32[16]{0:T(128)}, u32[]{:S(2)}) copy-start(f32[16]{0:T(128)} %param.9) | copy-start | bytes 196
Sparse Core Ops, SparseCore 0:
  192.9 172.4 all-reduce.1
